TPU v7x, 1024 devices: a whole 4x4x32 slice. The times are simulated.
1024 devices in a mesh: seq: 64 (over y, x, z_hi, core), head: 16 (over z_lo).
Axes of the slice: x: 4, y: 4, z: 32 (z_hi: 2, z_lo: 16; z = z_hi * 16 + z_lo), core: 2. Of those that a mesh axis runs over, the one named last changes fastest.
Arguments:
- queries: bfloat16 [16384, 8192], P(('seq', 'head')), may hold values from -0.125 to 0.125
- key_rows: bfloat16 [16384, 8192], P(('seq', 'head')), may hold values from -0.125 to 0.125
- value_rows: bfloat16 [16384, 8192], P(('seq', 'head')), may hold values from -0.125 to 0.125
- out_grad: bfloat16 [16384, 8192], P(('seq', 'head')), may hold values from -6 to 6
- log_decay: float32 [64, 16384], P('head', 'seq'), may hold values from -0.9 to 0, as said below
Outputs:
- query_grad: bfloat16 [16384, 8192], P(('seq', 'head'))
- key_grad: bfloat16 [16384, 8192], P(('seq', 'head'))
- value_grad: bfloat16 [16384, 8192], P(('seq', 'head'))
Inputs may be any that keep to these rules, and one draw needn't show every extreme that they name: `log_decay`: never positive.
All inputs are finite; a program needn't handle non-finite values.
Results may differ from a plain program's by a relative error of at most 0.0057.
Values may be sent and summed in bfloat16 or wider, within the bound.
A program may use at most 128 MiB of HBM per device.

v0:
```python
import jax
import jax.numpy as jnp
from jax import lax
from jax.sharding import PartitionSpec as P

HEAD_DIM = 128
BLOCK = 256


def prefix(shard, axis, combine, identity, reverse):
    peers, place = (lax.axis_size(axis), lax.axis_index(axis))
    everything = jax.tree.map(lambda part: lax.all_gather(part, axis), shard)
    start = jax.tree.map(
        lambda part, zero: jnp.broadcast_to(jnp.asarray(zero, part.dtype), part.shape),
        shard,
        identity,
    )

    def hop(k, before):
        at = peers - 1 - k if reverse else k
        reached = at > place if reverse else at < place
        new = combine(before, jax.tree.map(lambda part: part[at], everything))
        return jax.tree.map(lambda a, b: jnp.where(reached, a, b), new, before)

    return lax.fori_loop(0, peers, hop, start)


def compose(earlier, latter):
    gate_early, state_early = earlier
    gate_late, state_late = latter
    return (gate_early * gate_late, gate_late[..., None, None] * state_early + state_late)


def local_chain(block_gates, block_states, backward):

    def advance(running, element):
        return (compose(running, element), running)

    start_pair = (jnp.ones_like(block_gates[0]), jnp.zeros_like(block_states[0]))
    totals, before = lax.scan(advance, start_pair, (block_gates, block_states), reverse=backward)
    return (totals, before)


def head_major(rows, nblocks, heads_dev):
    return jnp.transpose(rows.reshape(nblocks, BLOCK, heads_dev, HEAD_DIM), (0, 2, 1, 3))


def row_major(blocks, seg_rows, heads_dev):
    return jnp.transpose(blocks, (0, 2, 1, 3)).reshape(seg_rows, heads_dev * HEAD_DIM)


def local(queries, key_rows, value_rows, out_grad, log_decay):
    heads_dev = log_decay.shape[0]
    seg_rows = log_decay.shape[1]
    nblocks = seg_rows // BLOCK
    query_heads, key_heads, value_heads, grad_heads = (
        lax.all_to_all(queries, "head", split_axis=1, concat_axis=0, tiled=True),
        lax.all_to_all(key_rows, "head", split_axis=1, concat_axis=0, tiled=True),
        lax.all_to_all(value_rows, "head", split_axis=1, concat_axis=0, tiled=True),
        lax.all_to_all(out_grad, "head", split_axis=1, concat_axis=0, tiled=True),
    )
    query_heads = head_major(query_heads, nblocks, heads_dev)
    key_heads = head_major(key_heads, nblocks, heads_dev)
    value_heads = head_major(value_heads, nblocks, heads_dev)
    grad_heads = head_major(grad_heads, nblocks, heads_dev)
    decay_blocks = jnp.transpose(log_decay.reshape(heads_dev, nblocks, BLOCK), (1, 0, 2))
    cumulative = jnp.cumsum(decay_blocks, axis=2)
    last_value = cumulative[:, :, -1:]
    query_weight = jnp.exp(cumulative)
    key_weight = jnp.exp(last_value - cumulative)
    block_gates = jnp.exp(last_value[:, :, 0])
    key_scaled = (key_heads.astype(jnp.float32) * key_weight[..., None]).astype(jnp.bfloat16)
    query_scaled = (query_heads.astype(jnp.float32) * query_weight[..., None]).astype(jnp.bfloat16)
    block_state = jnp.einsum(
        "nhbi,nhbj->nhij", key_scaled, value_heads, preferred_element_type=jnp.float32
    )
    block_grad = jnp.einsum(
        "nhbi,nhbj->nhij", query_scaled, grad_heads, preferred_element_type=jnp.float32
    )
    forward_total, forward_before = local_chain(block_gates, block_state, False)
    backward_total, backward_before = local_chain(block_gates, block_grad, True)
    identity_pair = (
        jnp.ones((heads_dev,), jnp.float32),
        jnp.zeros((heads_dev, HEAD_DIM, HEAD_DIM), jnp.float32),
    )
    incoming = prefix(forward_total, "seq", compose, identity_pair, False)[1]
    outgoing = prefix(backward_total, "seq", compose, identity_pair, True)[1]
    state_in = forward_before[0][:, :, None, None] * incoming[None] + forward_before[1]
    state_out = backward_before[0][:, :, None, None] * outgoing[None] + backward_before[1]
    state_in_low = state_in.astype(jnp.bfloat16)
    state_out_low = state_out.astype(jnp.bfloat16)
    token_positions = jnp.arange(BLOCK)
    causal = token_positions[:, None] >= token_positions[None, :]
    spread_log = cumulative[:, :, :, None] - cumulative[:, :, None, :]
    decay_matrix = jnp.where(causal, jnp.exp(jnp.where(causal, spread_log, 0.0)), 0.0)
    grad_scores = (
        jnp.einsum("nhti,nhsi->nhts", grad_heads, value_heads, preferred_element_type=jnp.float32)
        * decay_matrix
    ).astype(jnp.bfloat16)
    scores = (
        jnp.einsum("nhti,nhsi->nhts", query_heads, key_heads, preferred_element_type=jnp.float32)
        * decay_matrix
    ).astype(jnp.bfloat16)
    query_grad = jnp.einsum(
        "nhts,nhsi->nhti", grad_scores, key_heads, preferred_element_type=jnp.float32
    )
    query_grad = query_grad + query_weight[..., None] * jnp.einsum(
        "nhtj,nhij->nhti", grad_heads, state_in_low, preferred_element_type=jnp.float32
    )
    query_grad = row_major(query_grad.astype(jnp.bfloat16), seg_rows, heads_dev)
    key_grad = jnp.einsum(
        "nhts,nhti->nhsi", grad_scores, query_heads, preferred_element_type=jnp.float32
    )
    key_grad = key_grad + key_weight[..., None] * jnp.einsum(
        "nhsj,nhij->nhsi", value_heads, state_out_low, preferred_element_type=jnp.float32
    )
    key_grad = row_major(key_grad.astype(jnp.bfloat16), seg_rows, heads_dev)
    value_grad = jnp.einsum(
        "nhts,nhtj->nhsj", scores, grad_heads, preferred_element_type=jnp.float32
    )
    value_grad = value_grad + key_weight[..., None] * jnp.einsum(
        "nhsi,nhij->nhsj", key_heads, state_out_low, preferred_element_type=jnp.float32
    )
    value_grad = row_major(value_grad.astype(jnp.bfloat16), seg_rows, heads_dev)
    query_back, key_back, value_back = (
        lax.all_to_all(query_grad, "head", split_axis=0, concat_axis=1, tiled=True),
        lax.all_to_all(key_grad, "head", split_axis=0, concat_axis=1, tiled=True),
        lax.all_to_all(value_grad, "head", split_axis=0, concat_axis=1, tiled=True),
    )
    return (query_back, key_back, value_back)


def solution(mesh):
    return jax.shard_map(
        local,
        mesh=mesh,
        in_specs=(
            P(("seq", "head"), None),
            P(("seq", "head"), None),
            P(("seq", "head"), None),
            P(("seq", "head"), None),
            P("head", "seq"),
        ),
        out_specs=(P(("seq", "head"), None), P(("seq", "head"), None), P(("seq", "head"), None)),
        check_vma=False,
    )
```

profile of v0, /device:TPU:1, one launch (start us, length us, event | category | flops | bytes accessed | tf_op | source)
XLA Modules:
  0.0 1217.6 jit_solution(6697933359033008383)
XLA Ops:
  7.2 1.7 copy.176
  8.8 26.4 %all-to-all-start = ((bf16[16,16,512]{2,0,1:T(8,128)(2,1)}), bf16[16,16,512]{2,0,1:T(8,128)(2,1)S(1)}, u32[]{:S(2)}, u32[]{:S(2)}) async-start(bf16[16,16,512]{2,0,1:T(8,128)(2,1)} %bitcast.140), calls=%async_computation | async-start | bytes 524288 | tf_op jit(solution)/shard_map/all_to_all | solution.py:60
  35.3 1.7 copy.173
  37.0 25.0 %all-to-all-done = bf16[16,16,512]{2,0,1:T(8,128)(2,1)S(1)} async-done(((bf16[16,16,512]{2,0,1:T(8,128)(2,1)}), bf16[16,16,512]{2,0,1:T(8,128)(2,1)S(1)}, u32[]{:S(2)}, u32[]{:S(2)}) %all-to-all-start) | async-done | bytes 262176 | tf_op jit(solution)/shard_map/all_to_all | solution.py:60
  62.0 15.2 %all-to-all-start.4 = ((bf16[16,16,512]{2,0,1:T(8,128)(2,1)}), bf16[16,16,512]{2,0,1:T(8,128)(2,1)S(1)}, u32[]{:S(2)}, u32[]{:S(2)}) async-start(bf16[16,16,512]{2,0,1:T(8,128)(2,1)} %bitcast.137), calls=%async_computation.4 | async-start | bytes 524288 | tf_op jit(solution)/shard_map/all_to_all | solution.py:57
  78.0 1.2 reduce-window.6
  79.8 24.1 %all-to-all-done.4 = bf16[16,16,512]{2,0,1:T(8,128)(2,1)S(1)} async-done(((bf16[16,16,512]{2,0,1:T(8,128)(2,1)}), bf16[16,16,512]{2,0,1:T(8,128)(2,1)S(1)}, u32[]{:S(2)}, u32[]{:S(2)}) %all-to-all-start.4) | async-done | bytes 262176 | tf_op jit(solution)/shard_map/all_to_all | solution.py:57
  104.0 1.1 convolution_add_fusion
  105.2 1.7 copy.174
  106.9 15.3 %all-to-all-start.2 = ((bf16[16,16,512]{2,0,1:T(8,128)(2,1)}), bf16[16,16,512]{2,0,1:T(8,128)(2,1)S(1)}, u32[]{:S(2)}, u32[]{:S(2)}) async-start(bf16[16,16,512]{2,0,1:T(8,128)(2,1)} %bitcast.138), calls=%async_computation.2 | async-start | bytes 524288 | tf_op jit(solution)/shard_map/all_to_all | solution.py:58
  122.1 1.7 copy.175
  123.8 25.0 %all-to-all-done.2 = bf16[16,16,512]{2,0,1:T(8,128)(2,1)S(1)} async-done(((bf16[16,16,512]{2,0,1:T(8,128)(2,1)}), bf16[16,16,512]{2,0,1:T(8,128)(2,1)S(1)}, u32[]{:S(2)}, u32[]{:S(2)}) %all-to-all-start.2) | async-done | bytes 262176 | tf_op jit(solution)/shard_map/all_to_all | solution.py:58
  148.8 28.2 %all-to-all-start.1 = ((bf16[16,16,512]{2,0,1:T(8,128)(2,1)}), bf16[16,16,512]{2,0,1:T(8,128)(2,1)S(1)}, u32[]{:S(2)}, u32[]{:S(2)}) async-start(bf16[16,16,512]{2,0,1:T(8,128)(2,1)} %bitcast.139), calls=%async_computation.1 | async-start | bytes 524288 | tf_op jit(solution)/shard_map/all_to_all | solution.py:59
  177.2 26.6 %all-to-all-done.1 = bf16[16,16,512]{2,0,1:T(8,128)(2,1)S(1)} async-done(((bf16[16,16,512]{2,0,1:T(8,128)(2,1)}), bf16[16,16,512]{2,0,1:T(8,128)(2,1)S(1)}, u32[]{:S(2)}, u32[]{:S(2)}) %all-to-all-start.1) | async-done | bytes 262176 | tf_op jit(solution)/shard_map/all_to_all | solution.py:59
  203.8 1.1 convolution_add_fusion.1
  205.0 361.6 %all-gather = f32[64,4,1]{1,2,0:T(1,128)S(1)} all-gather(f32[1,4,1]{1,2,0:T(1,128)S(1)} %exp.47), channel_id=2, replica_groups=mesh['seq'=64,'head'=16] {'seq'}, dimensions={0}, use_global_device_ids=true | all-gather | bytes 1040 | tf_op jit(solution)/shard_map/all_gather | solution.py:12
  567.4 70.9 %while.21 = (s32[]{:T(128)}, f32[4,128,128]{2,1,0:T(8,128)S(1)}, s32[]{:T(128)}, f32[64,4]{1,0:T(8,128)S(1)}, f32[64,4,128,128]{3,2,1,0:T(8,128)}, /*index=5*/s32[]{:T(128)}, s32[]{:T(128)}, s32[]{:T(128)}, s32[]{:T(128)}) while((s32[]{:T(128)}, f32[4,128,128]{2,1,0:T(8,128)S(1)}, s32[]{:T(128)}, f32[64,4]{1,0:T(8,128)S(1)}, ...), condition=%wide.region_5.6_spmd.clone, body=%wide.region_4.5_spmd.clone.sunk | while | flops 262152 | bytes 786647 | solution.py:25
  567.4 1.1 fusion.70
  568.5 1.1 fusion.70
  569.6 1.1 fusion.70
  570.7 1.1 fusion.70
  571.8 1.1 fusion.70
  572.9 1.1 fusion.70
  574.0 1.1 fusion.70
  575.2 1.1 fusion.70
  576.3 1.1 fusion.70
  577.4 1.1 fusion.70
  578.5 1.1 fusion.70
  579.6 1.1 fusion.70
  580.7 1.1 fusion.70
  586.2 1.1 fusion.70
  594.0 1.1 fusion.70
  601.7 1.1 fusion.70
  602.8 1.1 fusion.70
  604.0 1.1 fusion.70
  605.1 1.1 fusion.70
  608.4 1.1 fusion.70
  613.9 1.1 fusion.70
  621.7 1.1 fusion.70
  629.4 1.1 fusion.70
  635.0 1.1 fusion.70
  640.2 59.7 %all-to-all-start.6 = ((bf16[16,16,512]{2,1,0:T(8,128)(2,1)}), bf16[16,16,512]{2,1,0:T(8,128)(2,1)S(1)}, u32[]{:S(2)}, u32[]{:S(2)}) async-start(bf16[16,16,512]{2,1,0:T(8,128)(2,1)} %all_to_all.110), calls=%async_computation.6 | async-start | bytes 524288 | tf_op jit(solution)/shard_map/all_to_all | solution.py:128
  699.9 289.2 %all-gather.6.cloned.1.call-done = f32[256,128,128]{2,1,0:T(8,128)} async-done(((f32[4,128,128]{2,1,0:T(8,128)}), f32[256,128,128]{2,1,0:T(8,128)}) %all-gather.6.cloned.1.call-update) | async-done | bytes 16777232 | tf_op jit(solution)/shard_map/all_gather | solution.py:12
  989.1 70.0 %while.20 = (s32[]{:T(128)}, f32[4,128,128]{2,1,0:T(8,128)S(1)}, s32[]{:T(128)}, f32[64,4]{1,0:T(8,128)S(1)}, f32[64,4,128,128]{3,2,1,0:T(8,128)}, /*index=5*/s32[]{:T(128)}, s32[]{:T(128)}) while((s32[]{:T(128)}, f32[4,128,128]{2,1,0:T(8,128)S(1)}, s32[]{:T(128)}, f32[64,4]{1,0:T(8,128)S(1)}, f32[64,4,128,128]{3,2,1,0:T(8,128)}, ...), condition=%wide.region_3.4_spmd.clone, body=%wide.region_2.3_spmd.clone.sunk | while | flops 262148 | bytes 786585 | solution.py:25
  1060.3 80.7 %all-to-all-start.3 = ((bf16[16,16,512]{2,1,0:T(8,128)(2,1)}), bf16[16,16,512]{2,1,0:T(8,128)(2,1)S(1)}, u32[]{:S(2)}, u32[]{:S(2)}) async-start(bf16[16,16,512]{2,1,0:T(8,128)(2,1)} %all_to_all.99), calls=%async_computation.3 | async-start | bytes 524288 | tf_op jit(solution)/shard_map/all_to_all | solution.py:126
  1142.6 26.1 %all-to-all-done.3 = bf16[16,16,512]{2,1,0:T(8,128)(2,1)S(1)} async-done(((bf16[16,16,512]{2,1,0:T(8,128)(2,1)}), bf16[16,16,512]{2,1,0:T(8,128)(2,1)S(1)}, u32[]{:S(2)}, u32[]{:S(2)}) %all-to-all-start.3) | async-done | bytes 262176 | tf_op jit(solution)/shard_map/all_to_all | solution.py:126
  1168.7 14.6 %all-to-all-start.5 = ((bf16[16,16,512]{2,1,0:T(8,128)(2,1)}), bf16[16,16,512]{2,1,0:T(8,128)(2,1)S(1)}, u32[]{:S(2)}, u32[]{:S(2)}) async-start(bf16[16,16,512]{2,1,0:T(8,128)(2,1)} %all_to_all.106), calls=%async_computation.5 | async-start | bytes 524288 | tf_op jit(solution)/shard_map/all_to_all | solution.py:127
  1184.8 25.3 %all-to-all-done.5 = bf16[16,16,512]{2,1,0:T(8,128)(2,1)S(1)} async-done(((bf16[16,16,512]{2,1,0:T(8,128)(2,1)}), bf16[16,16,512]{2,1,0:T(8,128)(2,1)S(1)}, u32[]{:S(2)}, u32[]{:S(2)}) %all-to-all-start.5) | async-done | bytes 262176 | tf_op jit(solution)/shard_map/all_to_all | solution.py:127
  (273 shorter events, 120.1 us)
Async XLA Ops:
  8.8 53.1 %all-to-all-start = ((bf16[16,16,512]{2,0,1:T(8,128)(2,1)}), bf16[16,16,512]{2,0,1:T(8,128)(2,1)S(1)}, u32[]{:S(2)}, u32[]{:S(2)}) async-start(bf16[16,16,512]{2,0,1:T(8,128)(2,1)} %bitcast.140), calls=%async_computation | async-start | bytes 524288 | tf_op jit(solution)/shard_map/all_to_all | solution.py:60
  62.0 41.9 %all-to-all-start.4 = ((bf16[16,16,512]{2,0,1:T(8,128)(2,1)}), bf16[16,16,512]{2,0,1:T(8,128)(2,1)S(1)}, u32[]{:S(2)}, u32[]{:S(2)}) async-start(bf16[16,16,512]{2,0,1:T(8,128)(2,1)} %bitcast.137), calls=%async_computation.4 | async-start | bytes 524288 | tf_op jit(solution)/shard_map/all_to_all | solution.py:57
  77.2 490.1 %all-gather.8.cloned.1.call-start = ((), (), s32[]{:S(2)}) async-start(), calls=%async_computation.8 | async-start | bytes 17039360 | tf_op jit(solution)/shard_map/all_gather | solution.py:12
  106.9 42.0 %all-to-all-start.2 = ((bf16[16,16,512]{2,0,1:T(8,128)(2,1)}), bf16[16,16,512]{2,0,1:T(8,128)(2,1)S(1)}, u32[]{:S(2)}, u32[]{:S(2)}) async-start(bf16[16,16,512]{2,0,1:T(8,128)(2,1)} %bitcast.138), calls=%async_computation.2 | async-start | bytes 524288 | tf_op jit(solution)/shard_map/all_to_all | solution.py:58
  148.8 54.9 %all-to-all-start.1 = ((bf16[16,16,512]{2,0,1:T(8,128)(2,1)}), bf16[16,16,512]{2,0,1:T(8,128)(2,1)S(1)}, u32[]{:S(2)}, u32[]{:S(2)}) async-start(bf16[16,16,512]{2,0,1:T(8,128)(2,1)} %bitcast.139), calls=%async_computation.1 | async-start | bytes 524288 | tf_op jit(solution)/shard_map/all_to_all | solution.py:59
  177.0 812.1 %all-gather.6.cloned.1.call-start = ((), (), s32[]{:S(2)}) async-start(), calls=%async_computation.7 | async-start | bytes 17039360 | tf_op jit(solution)/shard_map/all_gather | solution.py:12
  640.2 420.1 %all-to-all-start.6 = ((bf16[16,16,512]{2,1,0:T(8,128)(2,1)}), bf16[16,16,512]{2,1,0:T(8,128)(2,1)S(1)}, u32[]{:S(2)}, u32[]{:S(2)}) async-start(bf16[16,16,512]{2,1,0:T(8,128)(2,1)} %all_to_all.110), calls=%async_computation.6 | async-start | bytes 524288 | tf_op jit(solution)/shard_map/all_to_all | solution.py:128
  1060.3 108.4 %all-to-all-start.3 = ((bf16[16,16,512]{2,1,0:T(8,128)(2,1)}), bf16[16,16,512]{2,1,0:T(8,128)(2,1)S(1)}, u32[]{:S(2)}, u32[]{:S(2)}) async-start(bf16[16,16,512]{2,1,0:T(8,128)(2,1)} %all_to_all.99), calls=%async_computation.3 | async-start | bytes 524288 | tf_op jit(solution)/shard_map/all_to_all | solution.py:126
  1168.7 41.3 %all-to-all-start.5 = ((bf16[16,16,512]{2,1,0:T(8,128)(2,1)}), bf16[16,16,512]{2,1,0:T(8,128)(2,1)S(1)}, u32[]{:S(2)}, u32[]{:S(2)}) async-start(bf16[16,16,512]{2,1,0:T(8,128)(2,1)} %all_to_all.106), calls=%async_computation.5 | async-start | bytes 524288 | tf_op jit(solution)/shard_map/all_to_all | solution.py:127
Sparse Core Ops, SparseCore 0:
  105.3 442.3 all-gather.7
  554.0 435.0 all-gather.5
where the time goes:
time: 1230 us; the launch traced here: 1220 us
  waiting for transfers between devices  441 us (36%)
  blocking collectives  362 us (29%)
  starting transfers between devices  240 us (20%)
  other arithmetic  136 us (11%)
  local copies, waits for them, and re-layouts  14.5 us (1%)
  between operations  14.3 us (1%)
    all_gather x1, blocking collectives, prefix(): everything = jax.tree.map(lambda part: lax.all_gather(part, axis), shard)  362 us
    all_gather x2, waiting for transfers between devices, prefix(): everything = jax.tree.map(lambda part: lax.all_gather(part, axis), shard)  289 us
    select_n x128, other arithmetic, hop(): return jax.tree.map(lambda a, b: jnp.where(reached, a, b), new, before)  135 us
    all_to_all x1, starting transfers between devices, local(): lax.all_to_all(query_grad, 'head', split_axis=0, concat_axis=1, tiled=True)  80.7 us
    all_to_all x1, starting transfers between devices, local(): lax.all_to_all(value_grad, 'head', split_axis=0, concat_axis=1, tiled=True)  59.7 us
    all_to_all x1, starting transfers between devices, local(): lax.all_to_all(value_rows, 'head', split_axis=1, concat_axis=0, tiled=True)  28.2 us
    all_to_all x1, waiting for transfers between devices, local(): lax.all_to_all(value_rows, 'head', split_axis=1, concat_axis=0, tiled=True)  26.6 us
    all_to_all x1, starting transfers between devices, local(): lax.all_to_all(out_grad, 'head', split_axis=1, concat_axis=0, tiled=True)  26.4 us
  transfers between devices with their start and end apart: 9, of which 7 were waited for; matrix products, arithmetic and copies ran while one was open for 12% of the time, Pallas kernels for 0%

commit v1 on v0

v1 whole, which is shorter than its diff:
```python
import jax
import jax.numpy as jnp
from jax import lax
from jax.experimental import pallas as pl
from jax.experimental.pallas import tpu as pltpu
from jax.sharding import PartitionSpec as P

MESH = pl.DeviceIdType.MESH
F32 = jnp.float32
BF16 = jnp.bfloat16

DIM = 128
BLOCK = 256
ROWS = 16
LINE = 16
RING = 32
SIDE = 4
BLOCKS = 4
HEADS = 64
SLOTS = RING * 2
STATE = DIM + 8

K, V, G, Q = 0, 1, 2, 3
DQ, DK, DV = 0, 1, 2


def nt(a, b):
    return lax.dot_general(a, b, (((1,), (1,)), ((), ())), preferred_element_type=F32)


def nn(a, b):
    return lax.dot_general(a, b, (((1,), (0,)), ((), ())), preferred_element_type=F32)


def tn(a, b):
    return lax.dot_general(a, b, (((0,), (0,)), ((), ())), preferred_element_type=F32)


def kernel(
    q_in, k_in, v_in, g_in, decay_in, dq_out, dk_out, dv_out,
    stage, decay_own, decays, rows, back, result,
    decay_matrix, query_weight, key_weight, gates, scores,
    states, before, part_dk, part_dv,
    total_out, gather_x, row_out, gather_y,
    stage_sem, decay_sem, in_send, in_recv, out_send, out_recv, scan_send, scan_recv, final_sem,
):
    s, z_lo = lax.axis_index("seq"), lax.axis_index("head")
    y, x, z_hi, core = s // 16, (s // 4) % 4, (s // 2) % 2, s % 2
    base = (s // 4) * 4
    z = z_hi * LINE + z_lo
    my_block = z_hi * 2 + core
    my_slot = my_block * LINE + z_lo
    my_head = z_lo * BLOCKS + my_block

    def device(zz, cc):
        return (base + (zz // LINE) * 2 + cc, zz % LINE)

    def slot_of(zz, cc):
        return ((zz // LINE) * 2 + cc) * LINE + zz % LINE

    def head_of(zz, cc):
        return (zz % LINE) * BLOCKS + (zz // LINE) * 2 + cc

    def slot_rows(slot):
        return pl.ds(pl.multiple_of(slot * ROWS, ROWS), ROWS)

    def head_cols(head):
        return pl.ds(pl.multiple_of(head * DIM, DIM), DIM)

    sources = (k_in, v_in, g_in, q_in)
    for t in range(4):
        pltpu.make_async_copy(sources[t], stage.at[t], stage_sem.at[t]).start()
    decay_load = pltpu.make_async_copy(decay_in, decay_own, stage_sem.at[4])
    decay_load.start()

    barrier = pltpu.get_barrier_semaphore()

    def greet(i, carry):
        pl.semaphore_signal(
            barrier, inc=1, device_id=device((z + i // 2) % RING, (core + i) % 2), device_id_type=MESH
        )
        return carry

    lax.fori_loop(1, SLOTS, greet, 0)
    for step in range(1, SIDE):
        for peer in (y * 16 + ((x + step) % SIDE) * 4, ((y + step) % SIDE) * 16 + x * 4):
            pl.semaphore_signal(
                barrier, inc=1, device_id=(peer + my_block, z_lo), device_id_type=MESH
            )
    for t in range(4):
        pltpu.make_async_copy(sources[t], stage.at[t], stage_sem.at[t]).wait()
    decay_load.wait()
    pl.semaphore_wait(barrier, SLOTS - 1 + 2 * (SIDE - 1))

    def exchange(send):
        def both_ways(i, carry):
            far = LINE - i
            for cc in (0, 1):
                send((z + far) % RING, cc)

            @pl.when(far < LINE)
            def _():
                for cc in (0, 1):
                    send((z + RING - far) % RING, cc)

            return carry

        lax.fori_loop(0, LINE, both_ways, 0)
        send(z, 1 - core)

    def send_inputs(t):
        def send(zz, cc):
            pltpu.make_async_remote_copy(
                src_ref=stage.at[t].at[:, head_cols(head_of(zz, cc))],
                dst_ref=rows.at[t].at[slot_rows(my_slot)],
                send_sem=in_send.at[t],
                recv_sem=in_recv.at[t],
                device_id=device(zz, cc),
                device_id_type=MESH,
            ).start()

        exchange(send)
        pltpu.make_async_copy(
            stage.at[t].at[:, head_cols(my_head)], rows.at[t].at[slot_rows(my_slot)], in_recv.at[t]
        ).start()

    def send_outputs(t):
        def send(zz, cc):
            pltpu.make_async_remote_copy(
                src_ref=back.at[t].at[slot_rows(slot_of(zz, cc))],
                dst_ref=result.at[t].at[:, head_cols(my_head)],
                send_sem=out_send.at[t],
                recv_sem=out_recv.at[t],
                device_id=device(zz, cc),
                device_id_type=MESH,
            ).start()

        exchange(send)
        pltpu.make_async_copy(
            back.at[t].at[slot_rows(my_slot)], result.at[t].at[:, head_cols(my_head)], out_recv.at[t]
        ).start()

    def arrived(t):
        pltpu.make_async_copy(rows.at[t], rows.at[t], in_recv.at[t]).wait()

    for step in range(1, BLOCKS):
        peer = (my_block + step) % BLOCKS
        pltpu.make_async_remote_copy(
            src_ref=decay_own,
            dst_ref=decays.at[my_block],
            send_sem=decay_sem.at[0],
            recv_sem=decay_sem.at[1],
            device_id=(base + peer, z_lo),
            device_id_type=MESH,
        ).start()
    pltpu.make_async_copy(decay_own, decays.at[my_block], decay_sem.at[1]).start()
    for t in range(4):
        send_inputs(t)

    pltpu.make_async_copy(decays, decays, decay_sem.at[1]).wait()
    every = decays[...]
    wanted = lax.broadcasted_iota(jnp.int32, every.shape, 1) == my_block
    decay_rows = jnp.sum(jnp.where(wanted, every, 0.0), axis=1)
    upper = (
        lax.broadcasted_iota(jnp.int32, (BLOCK, BLOCK), 0)
        <= lax.broadcasted_iota(jnp.int32, (BLOCK, BLOCK), 1)
    ).astype(F32)
    padded = jnp.concatenate([decay_rows, jnp.zeros_like(decay_rows)], axis=0)
    cumulative = jnp.dot(
        padded, upper, preferred_element_type=F32, precision=lax.Precision.HIGHEST
    )
    time_at = lax.broadcasted_iota(jnp.int32, (BLOCK, DIM), 0)
    source_at = lax.broadcasted_iota(jnp.int32, (BLOCK, DIM), 1)
    for b in range(BLOCKS):
        row = cumulative[b : b + 1, :]
        column = jnp.transpose(jnp.broadcast_to(row, (DIM, BLOCK)))
        last = row[:, BLOCK - 1 : BLOCK]
        query_weight[b] = jnp.exp(column)
        key_weight[b] = jnp.exp(last - column)
        gates[b] = jnp.broadcast_to(jnp.exp(last), (8, DIM))
        for half in range(2):
            causal = time_at >= source_at + half * DIM
            spread = column - row[:, half * DIM : (half + 1) * DIM]
            decay_matrix[b, :, half * DIM : (half + 1) * DIM] = jnp.where(
                causal, jnp.exp(jnp.where(causal, spread, 0.0)), 0.0
            )

    def block(t, b):
        return rows[t, pl.ds(pl.multiple_of(b * BLOCK, BLOCK), BLOCK), :]

    def block_states(weight, left, right, which):
        def one(b, carry):
            scaled = (block(left, b).astype(F32) * weight[b]).astype(BF16)
            states[which, b] = tn(scaled, block(right, b))
            return carry

        lax.fori_loop(0, BLOCKS, one, 0)

    def scan_start(which, order):
        running = jnp.zeros((DIM, DIM), F32)
        gate = jnp.ones((8, DIM), F32)
        for b in order:
            here = gates[b]
            before[which, b, :DIM, :] = running
            before[which, b, DIM:, :] = gate
            running = here[:1] * running + states[which, b]
            gate = gate * here
        total_out[which, :DIM, :] = running
        total_out[which, DIM:, :] = gate
        gather_x[which, x, :DIM, :] = running
        gather_x[which, x, DIM:, :] = gate
        for step in range(1, SIDE):
            peer = y * 16 + ((x + step) % SIDE) * 4 + my_block
            pltpu.make_async_remote_copy(
                src_ref=total_out.at[which],
                dst_ref=gather_x.at[which].at[x],
                send_sem=scan_send.at[which].at[0],
                recv_sem=scan_recv.at[which].at[0],
                device_id=(peer, z_lo),
                device_id_type=MESH,
            ).start()

    def combined(gathered, which, place, order, backward):
        pre, pre_gate = jnp.zeros((DIM, DIM), F32), jnp.ones((8, DIM), F32)
        whole, whole_gate = pre, pre_gate
        for j in order:
            state, gate = gathered[which, j, :DIM, :], gathered[which, j, DIM:, :]
            earlier = j > place if backward else j < place
            pre = jnp.where(earlier, gate[:1] * pre + state, pre)
            pre_gate = jnp.where(earlier, gate * pre_gate, pre_gate)
            whole = gate[:1] * whole + state
            whole_gate = gate * whole_gate
        return pre, pre_gate, whole, whole_gate

    def wait_three(gathered, which, stage_index):
        three = gathered.at[which].at[pl.ds(0, SIDE - 1)]
        pltpu.make_async_copy(three, three, scan_recv.at[which].at[stage_index]).wait()

    def scan_finish(which, backward):
        order = tuple(reversed(range(SIDE))) if backward else tuple(range(SIDE))
        wait_three(gather_x, which, 0)
        pre, pre_gate, whole, whole_gate = combined(gather_x, which, x, order, backward)
        row_out[which, :DIM, :] = whole
        row_out[which, DIM:, :] = whole_gate
        gather_y[which, y, :DIM, :] = whole
        gather_y[which, y, DIM:, :] = whole_gate
        for step in range(1, SIDE):
            peer = ((y + step) % SIDE) * 16 + x * 4 + my_block
            pltpu.make_async_remote_copy(
                src_ref=row_out.at[which],
                dst_ref=gather_y.at[which].at[y],
                send_sem=scan_send.at[which].at[1],
                recv_sem=scan_recv.at[which].at[1],
                device_id=(peer, z_lo),
                device_id_type=MESH,
            ).start()
        wait_three(gather_y, which, 1)
        outer, _, _, _ = combined(gather_y, which, y, order, backward)
        return pre_gate[:1] * outer + pre

    arrived(K)
    arrived(V)
    block_states(key_weight, K, V, 0)
    scan_start(0, tuple(range(BLOCKS)))
    incoming = scan_finish(0, False)
    for b in range(BLOCKS):
        states[0, b] = before[0, b, DIM : DIM + 1, :] * incoming + before[0, b, :DIM, :]

    arrived(G)

    def query_block(b, carry):
        grad = block(G, b)
        low = (nt(grad, block(V, b)) * decay_matrix[b]).astype(BF16)
        scores[b] = low
        inner = nn(low, block(K, b))
        outer = query_weight[b] * nt(grad, states[0, b].astype(BF16))
        back[DQ, pl.ds(pl.multiple_of(b * BLOCK, BLOCK), BLOCK), :] = (inner + outer).astype(BF16)
        return carry

    lax.fori_loop(0, BLOCKS, query_block, 0)
    send_outputs(DQ)

    arrived(Q)
    block_states(query_weight, Q, G, 1)
    scan_start(1, tuple(reversed(range(BLOCKS))))

    def inner_block(b, carry):
        query, grad = block(Q, b), block(G, b)
        part_dk[b] = tn(scores[b], query)
        low = (nt(query, block(K, b)) * decay_matrix[b]).astype(BF16)
        part_dv[b] = tn(low, grad)
        return carry

    lax.fori_loop(0, BLOCKS, inner_block, 0)
    outgoing = scan_finish(1, True)
    for b in range(BLOCKS):
        states[1, b] = before[1, b, DIM : DIM + 1, :] * outgoing + before[1, b, :DIM, :]

    def key_block(b, carry):
        low = states[1, b].astype(BF16)
        grad = part_dk[b] + key_weight[b] * nt(block(V, b), low)
        back[DK, pl.ds(pl.multiple_of(b * BLOCK, BLOCK), BLOCK), :] = grad.astype(BF16)
        return carry

    lax.fori_loop(0, BLOCKS, key_block, 0)
    send_outputs(DK)

    def value_block(b, carry):
        low = states[1, b].astype(BF16)
        grad = part_dv[b] + key_weight[b] * nn(block(K, b), low)
        back[DV, pl.ds(pl.multiple_of(b * BLOCK, BLOCK), BLOCK), :] = grad.astype(BF16)
        return carry

    lax.fori_loop(0, BLOCKS, value_block, 0)
    send_outputs(DV)

    outs = (dq_out, dk_out, dv_out)
    for t in range(3):
        pltpu.make_async_copy(result.at[t], result.at[t], out_recv.at[t]).wait()
        pltpu.make_async_copy(result.at[t], outs[t], final_sem.at[t]).start()

    others = pl.ds(0, (SLOTS - 1) * ROWS)
    for t in range(4):
        sent = rows.at[t].at[others]
        pltpu.make_async_copy(sent, sent, in_send.at[t]).wait()
    for t in range(3):
        sent = back.at[t].at[others]
        pltpu.make_async_copy(sent, sent, out_send.at[t]).wait()
    three = decays.at[pl.ds(0, BLOCKS - 1)]
    pltpu.make_async_copy(three, three, decay_sem.at[0]).wait()
    for which in range(2):
        for stage_index, gathered in enumerate((gather_x, gather_y)):
            three = gathered.at[which].at[pl.ds(0, SIDE - 1)]
            pltpu.make_async_copy(three, three, scan_send.at[which].at[stage_index]).wait()
    for t in range(3):
        pltpu.make_async_copy(result.at[t], outs[t], final_sem.at[t]).wait()


def local(queries, key_rows, value_rows, out_grad, log_decay):
    shape = jax.ShapeDtypeStruct(queries.shape, BF16)
    anywhere = pl.BlockSpec(memory_space=pl.ANY)
    total = SLOTS * ROWS
    dma = pltpu.SemaphoreType.DMA
    return pl.pallas_call(
        kernel,
        out_shape=(shape,) * 3,
        in_specs=[anywhere] * 5,
        out_specs=(anywhere,) * 3,
        scratch_shapes=[
            pltpu.VMEM((4, ROWS, HEADS * DIM), BF16),
            pltpu.VMEM((BLOCKS, BLOCK), F32),
            pltpu.VMEM((BLOCKS, BLOCKS, BLOCK), F32),
            pltpu.VMEM((4, total, DIM), BF16),
            pltpu.VMEM((3, total, DIM), BF16),
            pltpu.VMEM((3, ROWS, HEADS * DIM), BF16),
            pltpu.VMEM((BLOCKS, BLOCK, BLOCK), F32),
            pltpu.VMEM((BLOCKS, BLOCK, DIM), F32),
            pltpu.VMEM((BLOCKS, BLOCK, DIM), F32),
            pltpu.VMEM((BLOCKS, 8, DIM), F32),
            pltpu.VMEM((BLOCKS, BLOCK, BLOCK), BF16),
            pltpu.VMEM((2, BLOCKS, DIM, DIM), F32),
            pltpu.VMEM((2, BLOCKS, STATE, DIM), F32),
            pltpu.VMEM((BLOCKS, BLOCK, DIM), F32),
            pltpu.VMEM((BLOCKS, BLOCK, DIM), F32),
            pltpu.VMEM((2, STATE, DIM), F32),
            pltpu.VMEM((2, SIDE, STATE, DIM), F32),
            pltpu.VMEM((2, STATE, DIM), F32),
            pltpu.VMEM((2, SIDE, STATE, DIM), F32),
            dma((5,)),
            dma((2,)),
            dma((4,)),
            dma((4,)),
            dma((3,)),
            dma((3,)),
            dma((2, 2)),
            dma((2, 2)),
            dma((3,)),
        ],
        compiler_params=pltpu.CompilerParams(collective_id=0, has_side_effects=True),
        name="attention_backward",
    )(queries, key_rows, value_rows, out_grad, log_decay)


def solution(mesh):
    rows = P(("seq", "head"), None)
    return jax.shard_map(
        local,
        mesh=mesh,
        in_specs=(rows, rows, rows, rows, P("head", "seq")),
        out_specs=(rows, rows, rows),
        check_vma=False,
    )
```

time: 1230 us -> 197 us (0.16)
  waiting for transfers between devices: 441 us -> 0 us
  blocking collectives: 362 us -> 0 us
  starting transfers between devices: 240 us -> 0 us
  Pallas kernels: 0 us -> 192 us
  other arithmetic: 136 us -> 0 us
  between operations: 14.3 us -> 0.65 us
    all_gather x1 -> x0, blocking collectives: 362 us -> none  [prefix(): everything = jax.tree.map(lambda part: lax.all_gather(part, axis), shard)]
    all_gather x2 -> x0, waiting for transfers between devices: 289 us -> none  [prefix(): everything = jax.tree.map(lambda part: lax.all_gather(part, axis), shard)]
    all_to_all x7 -> x0, starting transfers between devices: 240 us -> none  [the longest x1 80.7 us: local(): lax.all_to_all(query_grad, 'head', split_axis=0, concat_axis=1, tiled=True)]
    pallas_call x0 -> x1, Pallas kernels: none -> 192 us  [local(): pl.pallas_call(kernel, out_shape=(shape,) * 3, in_specs=[anywhere] * 5, o...]
    all_to_all x7 -> x0, waiting for transfers between devices: 152 us -> none  [the longest x1 26.6 us: local(): lax.all_to_all(value_rows, 'head', split_axis=1, concat_axis=0, tiled=True)]
    select_n x128 -> x0, other arithmetic: 135 us -> none  [hop(): return jax.tree.map(lambda a, b: jnp.where(reached, a, b), new, before)]
  transfers between devices with their start and end apart: 9 -> 0, of which waited for: 7 -> 0; matrix products, arithmetic and copies ran while one was open for 12% -> 0% of each run, Pallas kernels for 0% -> 0%
where the time goes in v1:
time: 197 us; the launch traced here: 196 us
  Pallas kernels  192 us (97%)
  local copies, waits for them, and re-layouts  3.46 us (2%)
    pallas_call x1, Pallas kernels, local(): pl.pallas_call(kernel, out_shape=(shape,) * 3, in_specs=[anywhere] * 5, o...  192 us

profile of v1, /device:TPU:1, one launch (start us, length us, event | category | flops | bytes accessed | tf_op | source)
XLA Modules:
  0.0 196.5 jit_solution(15147072571474840313)
XLA Ops:
  0.6 192.4 %attention_backward.1 = (bf16[16,8192]{1,0:T(8,128)(2,1)}, bf16[16,8192]{1,0:T(8,128)(2,1)}, bf16[16,8192]{1,0:T(8,128)(2,1)}) custom-call(bf16[16,8192]{1,0:T(8,128)(2,1)} %q_in.1, bf16[16,8192]{1,0:T(8,128)(2,1)} %k_in.1, bf16[16,8192]{1,0:T(8,128)(2,1)} %v_in.1, bf16[16,8192]{1,0:T(8,128)(2,1)} %g_in.1, f32[4,256]{1,0:T(4,128)} %decay_in.1), custom_call_target="tpu_custom_call" | custom-call | tf_op jit(solution)/shard_map/attention_backward/pallas_call | solution.py:344
  193.0 0.0 copy-start.1
  193.0 1.7 copy.11
  194.7 0.0 copy-done.1
  194.7 0.0 copy-start
  194.7 0.7 copy.12
  195.4 0.3 copy-done
  195.8 0.7 copy.13
Async XLA Ops:
  193.0 1.7 copy-start.1
  194.7 1.0 copy-start

commit v2 on v1

--- a/solution.py
+++ b/solution.py
@@ -38,11 +38,11 @@
 
 def kernel(
     q_in, k_in, v_in, g_in, decay_in, dq_out, dk_out, dv_out,
-    stage, decay_own, decays, rows, back, result,
+    stage, decay_own, decays, rows, back,
     decay_matrix, query_weight, key_weight, gates, scores,
     states, before, part_dk, part_dv,
     total_out, gather_x, row_out, gather_y,
-    stage_sem, decay_sem, in_send, in_recv, out_send, out_recv, scan_send, scan_recv, final_sem,
+    stage_sem, decay_sem, in_send, in_recv, out_send, out_recv, scan_send, scan_recv, left_sem, right_sem,
 ):
     s, z_lo = lax.axis_index("seq"), lax.axis_index("head")
     y, x, z_hi, core = s // 16, (s // 4) % 4, (s // 2) % 2, s % 2
@@ -68,6 +68,7 @@
         return pl.ds(pl.multiple_of(head * DIM, DIM), DIM)
 
     sources = (k_in, v_in, g_in, q_in)
+    results = (dq_out, dk_out, dv_out)
     for t in range(4):
         pltpu.make_async_copy(sources[t], stage.at[t], stage_sem.at[t]).start()
     decay_load = pltpu.make_async_copy(decay_in, decay_own, stage_sem.at[4])
@@ -75,22 +76,21 @@
 
     barrier = pltpu.get_barrier_semaphore()
 
-    def greet(i, carry):
-        pl.semaphore_signal(
-            barrier, inc=1, device_id=device((z + i // 2) % RING, (core + i) % 2), device_id_type=MESH
-        )
-        return carry
-
-    lax.fori_loop(1, SLOTS, greet, 0)
+    def greet(device_id):
+        pl.semaphore_signal(barrier, inc=1, device_id=device_id, device_id_type=MESH)
+
+    right, left = (z + 1) % RING, (z + RING - 1) % RING
+    for cc in (0, 1):
+        greet(device(right, cc))
+        greet(device(left, cc))
+    greet(device(z, 1 - core))
     for step in range(1, SIDE):
         for peer in (y * 16 + ((x + step) % SIDE) * 4, ((y + step) % SIDE) * 16 + x * 4):
-            pl.semaphore_signal(
-                barrier, inc=1, device_id=(peer + my_block, z_lo), device_id_type=MESH
-            )
+            greet((peer + my_block, z_lo))
     for t in range(4):
         pltpu.make_async_copy(sources[t], stage.at[t], stage_sem.at[t]).wait()
     decay_load.wait()
-    pl.semaphore_wait(barrier, SLOTS - 1 + 2 * (SIDE - 1))
+    pl.semaphore_wait(barrier, 5 + 2 * (SIDE - 1))
 
     def exchange(send):
         def both_ways(i, carry):
@@ -108,27 +108,52 @@
         lax.fori_loop(0, LINE, both_ways, 0)
         send(z, 1 - core)
 
-    def send_inputs(t):
-        def send(zz, cc):
-            pltpu.make_async_remote_copy(
-                src_ref=stage.at[t].at[:, head_cols(head_of(zz, cc))],
-                dst_ref=rows.at[t].at[slot_rows(my_slot)],
-                send_sem=in_send.at[t],
-                recv_sem=in_recv.at[t],
-                device_id=device(zz, cc),
-                device_id_type=MESH,
-            ).start()
-
-        exchange(send)
+    def send_input(t, zz, cc):
+        pltpu.make_async_remote_copy(
+            src_ref=stage.at[t].at[:, head_cols(head_of(zz, cc))],
+            dst_ref=rows.at[t].at[slot_rows(my_slot)],
+            send_sem=in_send.at[t],
+            recv_sem=in_recv.at[t],
+            device_id=device(zz, cc),
+            device_id_type=MESH,
+        ).start()
+
+    def keep_input(t):
         pltpu.make_async_copy(
             stage.at[t].at[:, head_cols(my_head)], rows.at[t].at[slot_rows(my_slot)], in_recv.at[t]
         ).start()
+
+    def farther(i, carry):
+        far = i + 1
+
+        @pl.when(far > 1)
+        def _():
+            pl.semaphore_wait(left_sem, 1)
+            pl.semaphore_wait(right_sem, 1)
+
+        @pl.when(far < LINE)
+        def _():
+            pl.semaphore_signal(left_sem, inc=1, device_id=device(right, core), device_id_type=MESH)
+            pl.semaphore_signal(right_sem, inc=1, device_id=device(left, core), device_id_type=MESH)
+
+        for t in (K, V):
+            for cc in (0, 1):
+                send_input(t, (z + far) % RING, cc)
+
+            @pl.when(far < LINE)
+            def _():
+                for cc in (0, 1):
+                    send_input(t, (z + RING - far) % RING, cc)
+
+        return carry
+
+    lax.fori_loop(0, LINE, farther, 0)
 
     def send_outputs(t):
         def send(zz, cc):
             pltpu.make_async_remote_copy(
                 src_ref=back.at[t].at[slot_rows(slot_of(zz, cc))],
-                dst_ref=result.at[t].at[:, head_cols(my_head)],
+                dst_ref=results[t].at[:, head_cols(my_head)],
                 send_sem=out_send.at[t],
                 recv_sem=out_recv.at[t],
                 device_id=device(zz, cc),
@@ -137,7 +162,7 @@
 
         exchange(send)
         pltpu.make_async_copy(
-            back.at[t].at[slot_rows(my_slot)], result.at[t].at[:, head_cols(my_head)], out_recv.at[t]
+            back.at[t].at[slot_rows(my_slot)], results[t].at[:, head_cols(my_head)], out_recv.at[t]
         ).start()
 
     def arrived(t):
@@ -154,8 +179,12 @@
             device_id_type=MESH,
         ).start()
     pltpu.make_async_copy(decay_own, decays.at[my_block], decay_sem.at[1]).start()
+    for t in (K, V):
+        send_input(t, z, 1 - core)
+    for t in (G, Q):
+        exchange(lambda zz, cc, t=t: send_input(t, zz, cc))
     for t in range(4):
-        send_inputs(t)
+        keep_input(t)
 
     pltpu.make_async_copy(decays, decays, decay_sem.at[1]).wait()
     every = decays[...]
@@ -314,10 +343,8 @@
     lax.fori_loop(0, BLOCKS, value_block, 0)
     send_outputs(DV)
 
-    outs = (dq_out, dk_out, dv_out)
     for t in range(3):
-        pltpu.make_async_copy(result.at[t], result.at[t], out_recv.at[t]).wait()
-        pltpu.make_async_copy(result.at[t], outs[t], final_sem.at[t]).start()
+        pltpu.make_async_copy(results[t], results[t], out_recv.at[t]).wait()
 
     others = pl.ds(0, (SLOTS - 1) * ROWS)
     for t in range(4):
@@ -332,8 +359,15 @@
         for stage_index, gathered in enumerate((gather_x, gather_y)):
             three = gathered.at[which].at[pl.ds(0, SIDE - 1)]
             pltpu.make_async_copy(three, three, scan_send.at[which].at[stage_index]).wait()
-    for t in range(3):
-        pltpu.make_async_copy(result.at[t], outs[t], final_sem.at[t]).wait()
+
+
+def place(dq_in, dk_in, dv_in, dq_out, dk_out, dv_out, sem):
+    pairs = ((dq_in, dq_out), (dk_in, dk_out), (dv_in, dv_out))
+    copies = [pltpu.make_async_copy(*pair, sem.at[t]) for t, pair in enumerate(pairs)]
+    for copy in copies:
+        copy.start()
+    for copy in copies:
+        copy.wait()
 
 
 def local(queries, key_rows, value_rows, out_grad, log_decay):
@@ -341,18 +375,21 @@
     anywhere = pl.BlockSpec(memory_space=pl.ANY)
     total = SLOTS * ROWS
     dma = pltpu.SemaphoreType.DMA
-    return pl.pallas_call(
+    held = [
+        pltpu.with_memory_space_constraint(array, pltpu.HBM)
+        for array in (queries, key_rows, value_rows, out_grad, log_decay)
+    ]
+    grads = pl.pallas_call(
         kernel,
         out_shape=(shape,) * 3,
-        in_specs=[anywhere] * 5,
-        out_specs=(anywhere,) * 3,
+        in_specs=[pl.BlockSpec(memory_space=pltpu.HBM)] * 5,
+        out_specs=(pl.BlockSpec(memory_space=pltpu.VMEM),) * 3,
         scratch_shapes=[
             pltpu.VMEM((4, ROWS, HEADS * DIM), BF16),
             pltpu.VMEM((BLOCKS, BLOCK), F32),
             pltpu.VMEM((BLOCKS, BLOCKS, BLOCK), F32),
             pltpu.VMEM((4, total, DIM), BF16),
             pltpu.VMEM((3, total, DIM), BF16),
-            pltpu.VMEM((3, ROWS, HEADS * DIM), BF16),
             pltpu.VMEM((BLOCKS, BLOCK, BLOCK), F32),
             pltpu.VMEM((BLOCKS, BLOCK, DIM), F32),
             pltpu.VMEM((BLOCKS, BLOCK, DIM), F32),
@@ -374,11 +411,23 @@
             dma((3,)),
             dma((2, 2)),
             dma((2, 2)),
-            dma((3,)),
+            pltpu.SemaphoreType.REGULAR,
+            pltpu.SemaphoreType.REGULAR,
         ],
-        compiler_params=pltpu.CompilerParams(collective_id=0, has_side_effects=True),
+        compiler_params=pltpu.CompilerParams(
+            collective_id=0, has_side_effects=True, vmem_limit_bytes=16 * 2**20
+        ),
         name="attention_backward",
-    )(queries, key_rows, value_rows, out_grad, log_decay)
+    )(*held)
+    return pl.pallas_call(
+        place,
+        out_shape=(shape,) * 3,
+        in_specs=[pl.BlockSpec(memory_space=pltpu.VMEM)] * 3,
+        out_specs=(anywhere,) * 3,
+        scratch_shapes=[dma((3,))],
+        compiler_params=pltpu.CompilerParams(vmem_limit_bytes=4 * 2**20),
+        name="place",
+    )(*grads)
 
 
 def solution(mesh):

time: 197 us -> 189 us (0.959)
  Pallas kernels: 192 us -> 188 us
  local copies, waits for them, and re-layouts: 3.46 us -> 0 us
    pallas_call x1 -> x2, Pallas kernels: 192 us -> 188 us  [the longest x1 187 us: local(): pl.pallas_call(kernel, out_shape=(shape,) * 3, in_specs=[pl.BlockSpec(mem...]
    unnamed x7 -> x0, local copies, waits for them, and re-layouts: 3.46 us -> none
where the time goes in v2:
time: 189 us
  Pallas kernels  188 us (99%)
    pallas_call x1, Pallas kernels, local(): pl.pallas_call(kernel, out_shape=(shape,) * 3, in_specs=[pl.BlockSpec(mem...  187 us

profile of v2, /device:TPU:1, one launch (start us, length us, event | category | flops | bytes accessed | tf_op | source)
XLA Modules:
  0.0 188.5 jit_solution(6650531187217913602)
XLA Ops:
  0.6 187.0 %attention_backward.1 = (bf16[16,8192]{1,0:T(8,128)(2,1)S(1)}, bf16[16,8192]{1,0:T(8,128)(2,1)S(1)}, bf16[16,8192]{1,0:T(8,128)(2,1)S(1)}) custom-call(bf16[16,8192]{1,0:T(8,128)(2,1)} %q_in.1, bf16[16,8192]{1,0:T(8,128)(2,1)} %k_in.1, bf16[16,8192]{1,0:T(8,128)(2,1)} %v_in.1, bf16[16,8192]{1,0:T(8,128)(2,1)} %g_in.1, f32[4,256]{1,0:T(4,128)} %decay_in.1), custom_call_target="tpu_custom_call" | custom-call | tf_op jit(solution)/shard_map/attention_backward/pallas_call | solution.py:382
  187.6 0.9 place.1

commit v3 on v2

--- a/solution.py
+++ b/solution.py
@@ -22,6 +22,8 @@
 
 K, V, G, Q = 0, 1, 2, 3
 DQ, DK, DV = 0, 1, 2
+EARLY = (DV,)
+EDGES = (0, 1, 2, 3, 4, 6, 8, 11, 32)
 
 
 def nt(a, b):
@@ -108,6 +110,28 @@
         lax.fori_loop(0, LINE, both_ways, 0)
         send(z, 1 - core)
 
+    def early_first(send):
+        for low, high in zip(EDGES[:-1], EDGES[1:]):
+
+            def both_ways(i, carry, low=low, high=high):
+                far = LINE - i
+                ahead, behind = (z + far) % RING, (z + RING - far) % RING
+
+                @pl.when((ahead >= low) & (ahead < high))
+                def _():
+                    for cc in (0, 1):
+                        send(ahead, cc)
+
+                @pl.when((far < LINE) & (behind >= low) & (behind < high))
+                def _():
+                    for cc in (0, 1):
+                        send(behind, cc)
+
+                return carry
+
+            lax.fori_loop(0, LINE, both_ways, 0)
+        send(z, 1 - core)
+
     def send_input(t, zz, cc):
         pltpu.make_async_remote_copy(
             src_ref=stage.at[t].at[:, head_cols(head_of(zz, cc))],
@@ -160,7 +184,7 @@
                 device_id_type=MESH,
             ).start()
 
-        exchange(send)
+        early_first(send) if t in EARLY else exchange(send)
         pltpu.make_async_copy(
             back.at[t].at[slot_rows(my_slot)], results[t].at[:, head_cols(my_head)], out_recv.at[t]
         ).start()

time: 189 us -> 184 us (0.974)
  Pallas kernels: 188 us -> 182 us
    pallas_call x1, Pallas kernels: 187 us -> 181 us  [local(): pl.pallas_call(kernel, out_shape=(shape,) * 3, in_specs=[pl.BlockSpec(mem...]
where the time goes in v3:
time: 184 us; the launch traced here: 183 us
  Pallas kernels  182 us (99%)
    pallas_call x1, Pallas kernels, local(): pl.pallas_call(kernel, out_shape=(shape,) * 3, in_specs=[pl.BlockSpec(mem...  181 us

profile of v3, /device:TPU:1, one launch (start us, length us, event | category | flops | bytes accessed | tf_op | source)
XLA Modules:
  0.0 182.7 jit_solution(12666325648606257122)
XLA Ops:
  0.6 181.2 %attention_backward.1 = (bf16[16,8192]{1,0:T(8,128)(2,1)S(1)}, bf16[16,8192]{1,0:T(8,128)(2,1)S(1)}, bf16[16,8192]{1,0:T(8,128)(2,1)S(1)}) custom-call(bf16[16,8192]{1,0:T(8,128)(2,1)} %q_in.1, bf16[16,8192]{1,0:T(8,128)(2,1)} %k_in.1, bf16[16,8192]{1,0:T(8,128)(2,1)} %v_in.1, bf16[16,8192]{1,0:T(8,128)(2,1)} %g_in.1, f32[4,256]{1,0:T(4,128)} %decay_in.1), custom_call_target="tpu_custom_call" | custom-call | tf_op jit(solution)/shard_map/attention_backward/pallas_call | solution.py:406
  181.8 0.9 place.1

commit v4 on v2

--- a/solution.py
+++ b/solution.py
@@ -22,6 +22,7 @@
 
 K, V, G, Q = 0, 1, 2, 3
 DQ, DK, DV = 0, 1, 2
+EDGES = (0, 1, 2, 3, 4, 5, 6, 8, 10)
 
 
 def nt(a, b):
@@ -149,7 +150,7 @@
 
     lax.fori_loop(0, LINE, farther, 0)
 
-    def send_outputs(t):
+    def output_sender(t):
         def send(zz, cc):
             pltpu.make_async_remote_copy(
                 src_ref=back.at[t].at[slot_rows(slot_of(zz, cc))],
@@ -160,7 +161,31 @@
                 device_id_type=MESH,
             ).start()
 
-        exchange(send)
+        return send
+
+    def send_range(t, low, high):
+        send = output_sender(t)
+
+        def both_ways(i, carry):
+            far = LINE - i
+            ahead, behind = (z + far) % RING, (z + RING - far) % RING
+
+            @pl.when((ahead >= low) & (ahead < high))
+            def _():
+                for cc in (0, 1):
+                    send(ahead, cc)
+
+            @pl.when((far < LINE) & (behind >= low) & (behind < high))
+            def _():
+                for cc in (0, 1):
+                    send(behind, cc)
+
+            return carry
+
+        lax.fori_loop(0, LINE, both_ways, 0)
+
+    def keep_output(t):
+        output_sender(t)(z, 1 - core)
         pltpu.make_async_copy(
             back.at[t].at[slot_rows(my_slot)], results[t].at[:, head_cols(my_head)], out_recv.at[t]
         ).start()
@@ -307,7 +332,8 @@
         return carry
 
     lax.fori_loop(0, BLOCKS, query_block, 0)
-    send_outputs(DQ)
+    send_range(DQ, 0, RING)
+    keep_output(DQ)
 
     arrived(Q)
     block_states(query_weight, Q, G, 1)
@@ -332,7 +358,15 @@
         return carry
 
     lax.fori_loop(0, BLOCKS, key_block, 0)
-    send_outputs(DK)
+    @pl.when(z_hi == 0)
+    def _():
+        send_range(DK, 0, RING)
+
+    @pl.when(z_hi == 1)
+    def _():
+        send_range(DK, 0, LINE)
+
+    keep_output(DK)
 
     def value_block(b, carry):
         low = states[1, b].astype(BF16)
@@ -341,7 +375,19 @@
         return carry
 
     lax.fori_loop(0, BLOCKS, value_block, 0)
-    send_outputs(DV)
+    for low, high in zip(EDGES[:-1], EDGES[1:]):
+        send_range(DV, low, high)
+
+    @pl.when(z_hi == 0)
+    def _():
+        send_range(DV, EDGES[-1], RING)
+
+    @pl.when(z_hi == 1)
+    def _():
+        send_range(DK, LINE, RING)
+        send_range(DV, EDGES[-1], RING)
+
+    keep_output(DV)
 
     for t in range(3):
         pltpu.make_async_copy(results[t], results[t], out_recv.at[t]).wait()

time: 189 us -> 185 us (0.979)
  the two profiles are of different devices: /device:TPU:1 before, /device:TPU:37 now
where the time goes in v4:
time: 185 us
  Pallas kernels  184 us (99%)
    pallas_call x1, Pallas kernels, local(): pl.pallas_call(kernel, out_shape=(shape,) * 3, in_specs=[pl.BlockSpec(mem...  183 us

profile of v4, /device:TPU:37, one launch (start us, length us, event | category | flops | bytes accessed | tf_op | source)
XLA Modules:
  0.0 185.0 jit_solution(12574027882857697602)
XLA Ops:
  0.6 183.4 %attention_backward.1 = (bf16[16,8192]{1,0:T(8,128)(2,1)S(1)}, bf16[16,8192]{1,0:T(8,128)(2,1)S(1)}, bf16[16,8192]{1,0:T(8,128)(2,1)S(1)}) custom-call(bf16[16,8192]{1,0:T(8,128)(2,1)} %q_in.1, bf16[16,8192]{1,0:T(8,128)(2,1)} %k_in.1, bf16[16,8192]{1,0:T(8,128)(2,1)} %v_in.1, bf16[16,8192]{1,0:T(8,128)(2,1)} %g_in.1, f32[4,256]{1,0:T(4,128)} %decay_in.1), custom_call_target="tpu_custom_call" | custom-call | tf_op jit(solution)/shard_map/attention_backward/pallas_call | solution.py:428
  184.1 0.9 place.1
